TPU v7x, 128 devices: a whole 4x4x4 slice. The times are simulated.
128 devices in a mesh: row: 32 (over z_lo, x, y), pair: 4 (over z_hi, core).
Axes of the slice: x: 4, y: 4, z: 4 (z_hi: 2, z_lo: 2; z = z_hi * 2 + z_lo), core: 2. Of those that a mesh axis runs over, the one named last changes fastest.
Arguments:
- snapshots: float32 [512, 4, 16384], P('row', 'pair'), may hold values from -6 to 6
- plan: int32 [2, 8], replicated, may hold values from 0 to 7, each once within a row
Outputs:
- rotated: float32 [512, 4, 16384], P(None, 'pair', 'row')
Inputs may be any that keep to these rules, and one draw needn't show every extreme that they name: Each row of plan names every block once.
All inputs are finite; a program needn't handle non-finite values.
Results may differ from a plain program's by a relative error of at most 0.00013.
Values sent between devices are 32-bit elements; how exact they have to be, the bound alone decides.
A program may use at most 128 MiB of HBM per device.

v0:
```python
import jax
import jax.numpy as jnp
from jax import lax
from jax.sharding import PartitionSpec as P


def matmul(left, right):
    return jnp.dot(left, right, precision=lax.Precision.HIGHEST, preferred_element_type=jnp.float32)


def cayley(scaled):
    order_size = scaled.shape[0]
    identity = jnp.eye(order_size, dtype=jnp.float32)
    system = identity + matmul(scaled.T, scaled)
    lifted = identity + scaled
    square = matmul(lifted, lifted)
    lower = lax.linalg.cholesky(system)
    middle = lax.linalg.triangular_solve(lower, square, left_side=True, lower=True)
    return lax.linalg.triangular_solve(lower, middle, left_side=True, lower=True, transpose_a=True)


def locate(current, wanted):
    slot_ids = jnp.arange(current.shape[0], dtype=jnp.int32)
    hits = current[None, :] == wanted[:, None]
    return jnp.sum(jnp.where(hits, slot_ids[None, :], 0), axis=1)


def relocate(work, current, target):
    pair_here = lax.axis_index("pair")
    pair_total = lax.axis_size("pair")
    block_width = work.shape[0] // 2
    row_count = work.shape[1]
    wanted = lax.dynamic_slice_in_dim(target, 2 * pair_here, 2)
    positions = locate(current, wanted)
    everything = lax.all_gather(work, "pair", axis=0, tiled=True).reshape(
        2 * pair_total, block_width, row_count
    )
    upper_block = lax.dynamic_index_in_dim(everything, positions[0], 0, keepdims=False)
    lower_block = lax.dynamic_index_in_dim(everything, positions[1], 0, keepdims=False)
    return jnp.concatenate([upper_block, lower_block], axis=0)


def rotate_whole(work):
    order_size = work.shape[0]
    gram = lax.psum(matmul(work, work.T), "row")
    scales = lax.rsqrt(jnp.diagonal(gram))
    normed = gram * scales[:, None] * scales[None, :]
    column_ids = jnp.arange(order_size, dtype=jnp.int32)
    signs = jnp.sign(column_ids[None, :] - column_ids[:, None]).astype(jnp.float32)
    skew = normed * signs
    factor = 1.0 + jnp.sqrt(jnp.sum(skew * skew))
    turn = cayley(skew / factor)
    return matmul(turn.T, work)


def on_device(snapshots, plan):
    arrived = lax.all_to_all(snapshots, "row", split_axis=2, concat_axis=0, tiled=True)
    work = arrived[:, 0, :]
    block_total = plan.shape[1]
    natural_order = jnp.arange(block_total, dtype=jnp.int32)
    current = natural_order
    for round_index in range(plan.shape[0]):
        target = plan[round_index]
        work = relocate(work, current, target)
        current = target
        work = rotate_whole(work)
    work = relocate(work, current, natural_order)
    return work[:, None, :]


def solution(mesh):
    in_specs = (P("row", "pair", None), P())
    out_specs = P(None, "pair", "row")
    return jax.shard_map(
        on_device, mesh=mesh, in_specs=in_specs, out_specs=out_specs, check_vma=False
    )
```

profile of v0, /device:TPU:1, one launch (start us, length us, event | category | flops | bytes accessed | tf_op | source)
XLA Modules:
  0.0 1240.9 jit_solution(9342640069578683527)
XLA Ops:
  6.5 15.5 %copy.30 = f32[16,1,16384]{0,1,2:T(1,128)} copy(f32[16,1,16384]{2,1,0:T(1,128)} %param.7) | data formatting | bytes 2097152 | tf_op args[0]
  22.6 74.5 %reduce.96 = f32[16384,16]{1,0:T(8,128)} reduce(f32[16384,1,16]{2,1,0:T(1,128)} %bitcast.161, f32[]{:T(128)} %broadcast.231), dimensions={1}, to_apply=%bitcast.125.reduce_sub_computation | reduce | bytes 2097156
  97.0 6.1 reshape.185
  103.1 24.7 %all_to_all.15 = f32[32,1,8192]{2,1,0:T(1,128)S(1)} all-to-all(f32[32,1,8192]{2,1,0:T(1,128)S(1)} %reshape.185), channel_id=1, replica_groups=mesh['row'=32,'pair'=4] {'row'}, dimensions={0} | all-to-all | bytes 2097152 | tf_op jit(solution)/shard_map/all_to_all | solution.py:57
  131.1 17.3 %reshape.186 = f32[16384,1,16]{2,1,0:T(1,128)} reshape(f32[32,8192]{1,0:T(8,128)S(1)} %reduce.97) | data formatting | bytes 2097152
  148.3 5.3 copy.37
  160.7 34.6 %all-gather.4.cloned.1.call-done = f32[2048,512]{1,0:T(8,128)} async-done(((f32[512,512]{1,0:T(8,128)}), f32[2048,512]{1,0:T(8,128)}) %all-gather.4.cloned.1.call-update) | async-done | bytes 4194320 | tf_op jit(solution)/shard_map/all_gather | solution.py:35
  201.1 287.3 %all-reduce.4.cloned.1.call-done = f32[512,512]{1,0:T(8,128)} async-done(((f32[512,512]{1,0:T(8,128)}), f32[512,512]{1,0:T(8,128)}) %all-reduce.4.cloned.1.call-update) | async-done | bytes 1048592 | tf_op jit(solution)/shard_map/psum | solution.py:45
  488.4 8.6 gather_fusion
  499.9 3.9 fusion.139
  504.4 11.7 custom-call.43
  516.7 9.8 custom-call.44
  527.6 12.7 %custom-call.45 = f32[128,128]{1,0:T(8,128)} custom-call(f32[128,128]{1,0:T(8,128)S(1)} %slice.298), custom_call_target="Cholesky" | custom-call | tf_op jit(solution)/shard_map/cholesky/custom-call.5 | solution.py:17
  542.8 9.8 custom-call.46
  553.2 11.7 custom-call.47
  565.0 9.8 custom-call.48
  575.4 11.9 custom-call.49
  593.8 7.9 while.8
  601.7 39.3 %custom-call.51 = f32[4,128,128]{1,2,0:T(8,128)S(1)} custom-call(f32[4,128,128]{2,1,0:T(8,128)S(1)} %get-tuple-element.37), custom_call_target="InvertDiagBlocksLowerTriangular" | custom-call | tf_op jit(solution)/shard_map/triangular_solve/custom-call.8 | solution.py:19
  657.1 57.0 %all-gather.6.cloned.1.call-done = f32[2048,512]{1,0:T(8,128)} async-done(((f32[512,512]{1,0:T(8,128)}), f32[2048,512]{1,0:T(8,128)}) %all-gather.6.cloned.1.call-update) | async-done | bytes 4194320 | tf_op jit(solution)/shard_map/all_gather | solution.py:35
  719.3 287.8 %all-reduce.6.cloned.1.call-done = f32[512,512]{1,0:T(8,128)} async-done(((f32[512,512]{1,0:T(8,128)}), f32[512,512]{1,0:T(8,128)}) %all-reduce.6.cloned.1.call-update) | async-done | bytes 1048592 | tf_op jit(solution)/shard_map/psum | solution.py:45
  1007.2 8.8 gather_fusion.1
  1023.4 11.7 custom-call.52
  1035.7 9.8 custom-call.53
  1046.6 12.5 %custom-call.54 = f32[128,128]{1,0:T(8,128)} custom-call(f32[128,128]{1,0:T(8,128)S(1)} %slice.325), custom_call_target="Cholesky" | custom-call | tf_op jit(solution)/shard_map/cholesky/custom-call.5 | solution.py:17
  1061.0 9.8 custom-call.55
  1071.5 11.7 custom-call.56
  1083.2 9.8 custom-call.57
  1093.6 11.9 custom-call.58
  1110.8 7.9 while.9
  1118.7 39.3 %custom-call.60 = f32[4,128,128]{1,2,0:T(8,128)S(1)} custom-call(f32[4,128,128]{2,1,0:T(8,128)S(1)} %get-tuple-element.39), custom_call_target="InvertDiagBlocksLowerTriangular" | custom-call | tf_op jit(solution)/shard_map/triangular_solve/custom-call.8 | solution.py:19
  1174.1 57.0 %all-gather.8.cloned.1.call-done = f32[2048,512]{1,0:T(8,128)} async-done(((f32[512,512]{1,0:T(8,128)}), f32[2048,512]{1,0:T(8,128)}) %all-gather.8.cloned.1.call-update) | async-done | bytes 4194320 | tf_op jit(solution)/shard_map/all_gather | solution.py:35
  (170 shorter events, 86.9 us)
Async XLA Ops:
  6.5 188.8 %all-gather.4.cloned.1.call-start = ((), (), s32[]{:S(2)}) async-start(), calls=%async_computation.1 | async-start | bytes 5242880 | tf_op jit(solution)/shard_map/all_gather | solution.py:35
  148.3 6.9 copy-start.12
  155.2 333.2 %all-reduce.4.cloned.1.call-start = ((), (), s32[]{:S(2)}) async-start(), calls=%async_computation.2 | async-start | bytes 2097152 | tf_op jit(solution)/shard_map/psum | solution.py:45
  196.6 0.8 copy-start.6
  196.6 1.0 copy-start.8
  200.5 513.6 %all-gather.6.cloned.1.call-start = ((), (), s32[]{:S(2)}) async-start(), calls=%async_computation.3 | async-start | bytes 5242880 | tf_op jit(solution)/shard_map/all_gather | solution.py:35
  516.1 0.6 copy-start.10
  526.5 114.5 %copy-start.1 = (f32[512,512]{1,0:T(8,128)S(1)}, f32[512,512]{1,0:T(8,128)}, u32[]{:S(2)}) copy-start(f32[512,512]{1,0:T(8,128)} %all-reduce.4.cloned.1.call-done) | copy-start | bytes 3145732
  645.0 4.6 copy-start.7
  645.0 4.6 copy-start.9
  652.5 354.7 %all-reduce.6.cloned.1.call-start = ((), (), s32[]{:S(2)}) async-start(), calls=%async_computation.4 | async-start | bytes 2097152 | tf_op jit(solution)/shard_map/psum | solution.py:45
  715.4 0.8 copy-start.2
  715.4 1.0 copy-start.4
  719.3 511.9 %all-gather.8.cloned.1.call-start = ((), (), s32[]{:S(2)}) async-start(), calls=%async_computation.5 | async-start | bytes 5242880 | tf_op jit(solution)/shard_map/all_gather | solution.py:35
  1035.1 0.6 copy-start.11
  1045.5 112.5 %copy-start = (f32[512,512]{1,0:T(8,128)S(1)}, f32[512,512]{1,0:T(8,128)}, u32[]{:S(2)}) copy-start(f32[512,512]{1,0:T(8,128)} %all-reduce.6.cloned.1.call-done) | copy-start | bytes 3145732
  1162.0 4.6 copy-start.3
  1162.0 4.6 copy-start.5
  1164.7 4.9 copy-start.13
Sparse Core Ops, SparseCore 0:
  155.3 39.9 all-gather.3
  200.6 287.7 all-reduce.3
  652.6 61.4 all-gather.5
  719.4 287.7 all-reduce.5
  1169.6 61.4 all-gather.7
where the time goes:
time: 1250 us; the launch traced here: 1240 us
  waiting for transfers between devices  724 us (58%)
  other arithmetic  325 us (26%)
  local copies, waits for them, and re-layouts  94.2 us (8%)
  matrix products  40.3 us (3%)
  between operations  32 us (3%)
  blocking collectives  24.7 us (2%)
    psum x2, waiting for transfers between devices, rotate_whole(): gram = lax.psum(matmul(work, work.T), 'row')  575 us
    another operation x30, other arithmetic, cayley(): lower = lax.linalg.cholesky(system)  163 us
    all_gather x3, waiting for transfers between devices, relocate(): lax.all_gather(work, 'pair', axis=0, tiled=True)  149 us
    another operation x5, other arithmetic, cayley(): lax.linalg.triangular_solve(lower, middle, left_side=True, lower=True, tr...  79.4 us
    unnamed x1, other arithmetic  74.5 us
    unnamed x32, local copies, waits for them, and re-layouts  42.6 us
  transfers between devices with their start and end apart: 5, of which 5 were waited for; matrix products, arithmetic and copies ran while one was open for 0% of the time, Pallas kernels for 0%

commit v1 on v0

v1 whole, which is shorter than its diff:
```python
import functools

import jax
import jax.numpy as jnp
from jax import lax
from jax.experimental import pallas as pl
from jax.experimental.pallas import tpu as pltpu
from jax.sharding import PartitionSpec as P

MESH = pl.DeviceIdType.MESH
F32 = jnp.float32
BF16 = jnp.bfloat16
NN = (((1,), (0,)), ((), ()))
NT = (((1,), (1,)), ((), ()))
TILES = [(i, j) for i in range(4) for j in range(i, 4)]
TILE_ROWS = 128 * len(TILES)
T2_AT, T4_AT, T8_AT = 49.0, 4801.0, 46099201.0
INVERSE_SCALE = 32.0 * 5.0 * T2_AT * T4_AT / T8_AT


def dot(left, right, dims=NN):
    return lax.dot_general(left, right, dims, preferred_element_type=F32)


def split(value):
    high = value.astype(BF16)
    return high, (value - high.astype(F32)).astype(BF16)


def dot3(left, right, dims=NN):
    (left_high, left_low), (right_high, right_low) = left, right
    return (
        dot(left_high, right_high, dims)
        + dot(left_high, right_low, dims)
        + dot(left_low, right_high, dims)
    )


def identity(size):
    shape = (size, size)
    return lax.broadcasted_iota(jnp.int32, shape, 0) == lax.broadcasted_iota(jnp.int32, shape, 1)


def kernel(n_row, table, snap, out, S0, S1, S2, E, RSB, RED, G, f0, f1, h0, l0, h1, l1, h2, l2, h3,
           sem_in, sem_in_s, sem_sw, sem_sw_s, sem_rs, sem_rs_s, sem_ag, sem_ag_s):
    r = lax.axis_index("row")
    p = lax.axis_index("pair")
    h, c = p // 2, p % 2
    n_peer = 2 * n_row
    me = h * n_row + r
    part = TILE_ROWS // n_row
    order = 512
    half = 256
    S = (S0, S1, S2)
    width = S0.shape[2]
    own = snap.shape[0]
    partner = (r, 2 * h + 1 - c)

    def peer_of(k):
        peer = lax.rem(me + k, n_peer)
        return lax.rem(peer, n_row), peer // n_row

    barrier = pltpu.get_barrier_semaphore()

    def greet(k, carry):
        pr, ph = peer_of(k)
        pl.semaphore_signal(barrier, inc=1, device_id=(pr, 2 * ph + c), device_id_type=MESH)
        return carry

    pl.semaphore_signal(barrier, inc=1, device_id=partner, device_id_type=MESH)
    lax.fori_loop(1, n_peer, greet, 0)
    pl.semaphore_wait(barrier, n_peer)

    mine = S0.at[2 * p + (own * r) // half, pl.ds(pl.multiple_of(lax.rem(own * r, half), own), own), :]
    local = pltpu.make_async_copy(
        snap.at[:, 0, pl.ds(pl.multiple_of(width * r, width), width)], mine, sem_in.at[h])
    local.start()

    def scatter(k, carry):
        pr, ph = peer_of(k)
        pltpu.make_async_remote_copy(
            src_ref=snap.at[:, 0, pl.ds(pl.multiple_of(width * pr, width), width)],
            dst_ref=mine,
            send_sem=sem_in_s, recv_sem=sem_in.at[h],
            device_id=(pr, 2 * ph + c), device_id_type=MESH).start()
        return carry

    lax.fori_loop(1, n_peer, scatter, 0)

    def blocks_of(s, q):
        return S[s].at[pl.ds(2 * q, 2)]

    def swap(s, hq):
        q = 2 * hq + c
        return pltpu.make_async_remote_copy(
            src_ref=blocks_of(s, q), dst_ref=blocks_of(s, q),
            send_sem=sem_sw_s.at[s, hq], recv_sem=sem_sw.at[s, hq],
            device_id=partner, device_id_type=MESH)

    def await_bytes(ref, sem):
        pltpu.make_async_copy(ref, ref, sem).wait()

    def await_swap(s):
        for hq in range(2):
            other = blocks_of(s, 2 * hq + 1 - c)
            await_bytes(other, sem_sw.at[s, hq])
            await_bytes(other, sem_sw_s.at[s, hq])

    for hq in range(2):
        await_bytes(blocks_of(0, 2 * hq + c), sem_in.at[hq])
        swap(0, hq).start()
    await_bytes(S0.at[pl.ds(0, 6), pl.ds(0, own * (n_peer - 1) // 6), :], sem_in_s)
    await_swap(0)

    eye = identity(order)

    def load_pair(s, q):
        parts = [S[s][table[s, 2 * q + side]] for side in range(2)]
        return split(jnp.concatenate(parts, axis=0))

    def one_round(s):
        h0[...], l0[...] = load_pair(s, p)
        pair = (h0[...], l0[...])
        gram = dot3(pair, pair, NT)
        for n, (i, j) in enumerate(TILES):
            E[s, pl.ds(128 * n, 128), :] = gram[128 * i:128 * i + 128, 128 * j:128 * j + 128]

        def slice_of(k):
            return pl.ds(pl.multiple_of(part * k, part), part)

        def reduce_send(k, c2):
            pr = lax.rem(r + k, n_row)
            pltpu.make_async_remote_copy(
                src_ref=E.at[s, slice_of(pr), :], dst_ref=RSB.at[s, slice_of(r), :],
                send_sem=sem_rs_s.at[s], recv_sem=sem_rs.at[s],
                device_id=(pr, p), device_id_type=MESH).start()
            return c2

        pltpu.make_async_copy(E.at[s, slice_of(r), :], RSB.at[s, slice_of(r), :], sem_rs.at[s]).start()
        lax.fori_loop(1, n_row, reduce_send, 0)
        await_bytes(RSB.at[s], sem_rs.at[s])
        total = jnp.zeros((part, 128), F32)
        for k in range(n_row):
            total = total + RSB[s, pl.ds(part * k, part), :]
        RED[s] = total
        await_bytes(E.at[s, pl.ds(0, part * (n_row - 1)), :], sem_rs_s.at[s])

        def gather_send(k, c2):
            pr, ph = peer_of(k)
            pltpu.make_async_remote_copy(
                src_ref=RED.at[s], dst_ref=G.at[s, slice_of(h * n_row + r), :],
                send_sem=sem_ag_s.at[s], recv_sem=sem_ag.at[s, h],
                device_id=(pr, 2 * ph + c), device_id_type=MESH).start()
            return c2

        pltpu.make_async_copy(RED.at[s], G.at[s, slice_of(h * n_row + r), :], sem_ag.at[s, h]).start()
        lax.fori_loop(1, n_peer, gather_send, 0)

        def rotate(hq, c2):
            base = pl.multiple_of(TILE_ROWS * hq, TILE_ROWS)
            await_bytes(G.at[s, pl.ds(base, TILE_ROWS), :], sem_ag.at[s, hq])
            tile = {ij: G[s, pl.ds(base + 128 * n, 128), :] for n, ij in enumerate(TILES)}
            on = identity(128)
            columns, rows = [], []
            for i in range(4):
                diagonal = jnp.where(on, tile[i, i], 0.0)
                columns.append(lax.rsqrt(jnp.sum(diagonal, axis=1, keepdims=True)))
                rows.append(lax.rsqrt(jnp.sum(diagonal, axis=0, keepdims=True)))
            row_ids = lax.broadcasted_iota(jnp.int32, (128, 128), 0)
            column_ids = lax.broadcasted_iota(jnp.int32, (128, 128), 1)
            signs = jnp.where(column_ids > row_ids, 1.0, jnp.where(column_ids < row_ids, -1.0, 0.0))
            squares = jnp.zeros((128, 128), F32)
            skew = {}
            for i, j in TILES:
                normed = tile[i, j] * columns[i] * rows[j]
                if i == j:
                    normed = normed * signs
                    squares = squares + normed * normed
                else:
                    squares = squares + 2.0 * (normed * normed)
                skew[i, j] = normed
            scale = 1.0 / (1.0 + jnp.sqrt(jnp.sum(squares, keepdims=True)))
            for i, j in TILES:
                scaled = skew[i, j] * scale
                f0[pl.ds(128 * i, 128), pl.ds(128 * j, 128)] = scaled
                if i != j:
                    f0[pl.ds(128 * j, 128), pl.ds(128 * i, 128)] = -scaled.T
            h0[...], l0[...] = split(f0[...])
            a = (h0[...], l0[...])
            f1[...] = 4.0 * dot3(a, a) + jnp.where(eye, 1.0, 0.0)
            h1[...], l1[...] = split(f1[...])
            w = (h1[...], l1[...])
            h2[...], l2[...] = split(2.0 * dot3(w, w) - jnp.where(eye, 1.0, 0.0))
            t2 = (h2[...], l2[...])
            h3[...] = (2.0 * dot(h2[...], h2[...]) - jnp.where(eye, 1.0, 0.0)).astype(BF16)
            f0[...] = jnp.where(eye, 1.0, 0.0) - f0[...] + 0.2 * (f1[...] - dot3(a, w))
            h0[...], l0[...] = split(f0[...])
            f0[...] = f0[...] + (1.0 / T2_AT) * dot3((h0[...], l0[...]), t2)
            h0[...] = f0[...].astype(BF16)
            f0[...] = f0[...] + (1.0 / T4_AT) * dot(h0[...], h3[...])
            h0[...], l0[...] = split((2.0 * INVERSE_SCALE) * f0[...] - jnp.where(eye, 1.0, 0.0))
            q = 2 * hq + c
            h1[...], l1[...] = load_pair(s, q)
            turned = dot3((h0[...], l0[...]), (h1[...], l1[...]))
            for side in range(2):
                S[s + 1][2 * q + side] = turned[half * side:half * side + half]
            swap(s + 1, hq).start()
            return c2

        lax.fori_loop(0, 2, rotate, 0)
        await_bytes(G.at[s, pl.ds(0, part * (n_peer - 1)), :], sem_ag_s.at[s])
        await_swap(s + 1)

    one_round(0)
    one_round(1)
    for side in range(2):
        out[pl.ds(half * side, half), :] = S2[table[2, 2 * p + side]]


def places(plan):
    natural = jnp.arange(plan.shape[1], dtype=jnp.int32)
    wanted = jnp.stack([plan[1], natural])
    hits = plan[:, None, :] == wanted[:, :, None]
    found = jnp.sum(jnp.where(hits, natural, 0), axis=2)
    return jnp.concatenate([plan[:1], found], axis=0)


def on_device(n_row, snapshots, plan):
    width = snapshots.shape[2] // n_row
    part = TILE_ROWS // n_row
    dma = pltpu.SemaphoreType.DMA
    full = (512, 512)
    result = pl.pallas_call(
        functools.partial(kernel, n_row),
        out_shape=jax.ShapeDtypeStruct((512, width), F32),
        in_specs=[pl.BlockSpec(memory_space=pltpu.SMEM), pl.BlockSpec(memory_space=pl.ANY)],
        out_specs=pl.BlockSpec(memory_space=pltpu.VMEM),
        scratch_shapes=[
            pltpu.VMEM((8, 256, width), F32), pltpu.VMEM((8, 256, width), F32), pltpu.VMEM((8, 256, width), F32),
            pltpu.VMEM((2, TILE_ROWS, 128), F32),
            pltpu.VMEM((2, TILE_ROWS, 128), F32),
            pltpu.VMEM((2, part, 128), F32),
            pltpu.VMEM((2, 2 * TILE_ROWS, 128), F32),
            pltpu.VMEM(full, F32), pltpu.VMEM(full, F32),
            pltpu.VMEM(full, BF16), pltpu.VMEM(full, BF16), pltpu.VMEM(full, BF16), pltpu.VMEM(full, BF16),
            pltpu.VMEM(full, BF16), pltpu.VMEM(full, BF16), pltpu.VMEM(full, BF16),
            dma((2,)), dma, dma((3, 2)), dma((3, 2)), dma((2,)), dma((2,)), dma((2, 2)), dma((2,)),
        ],
        compiler_params=pltpu.CompilerParams(
            collective_id=0, has_side_effects=True, vmem_limit_bytes=60 * 1024 * 1024),
    )(places(plan), snapshots)
    return result[:, None, :]


def solution(mesh):
    n_row = mesh.shape["row"]
    return jax.shard_map(
        functools.partial(on_device, n_row), mesh=mesh,
        in_specs=(P("row", "pair", None), P()), out_specs=P(None, "pair", "row"), check_vma=False)
```

time: 1250 us -> 145 us (0.12)
  waiting for transfers between devices: 724 us -> 0 us
  other arithmetic: 325 us -> 0.82 us
  Pallas kernels: 0 us -> 140 us
  local copies, waits for them, and re-layouts: 94.2 us -> 3.95 us
  matrix products: 40.3 us -> 0 us
  between operations: 32 us -> 0.01 us
  blocking collectives: 24.7 us -> 0 us
    psum x2 -> x0, waiting for transfers between devices: 575 us -> none  [rotate_whole(): gram = lax.psum(matmul(work, work.T), 'row')]
    another operation x35 -> x1, other arithmetic: 242 us -> 0.01 us  [places(): wanted = jnp.stack([plan[1], natural])]
    all_gather x3 -> x0, waiting for transfers between devices: 149 us -> none  [relocate(): lax.all_gather(work, 'pair', axis=0, tiled=True)]
    pallas_call x0 -> x1, Pallas kernels: none -> 140 us  [on_device(): pl.pallas_call(functools.partial(kernel, n_row), out_shape=jax.ShapeDtype...]
    unnamed x1 -> x0, other arithmetic: 74.5 us -> none
    unnamed x32 -> x2, local copies, waits for them, and re-layouts: 42.6 us -> 0.67 us
    all_to_all x1 -> x0, blocking collectives: 24.7 us -> none  [on_device(): lax.all_to_all(snapshots, 'row', split_axis=2, concat_axis=0, tiled=True)]
    dot_general x8 -> x0, matrix products: 23.7 us -> none  [matmul(): jnp.dot(left, right, precision=lax.Precision.HIGHEST, preferred_element_t...]
  transfers between devices with their start and end apart: 5 -> 0, of which waited for: 5 -> 0; matrix products, arithmetic and copies ran while one was open for 0% -> 0% of each run, Pallas kernels for 0% -> 0%
where the time goes in v1:
time: 145 us
  Pallas kernels  140 us (97%)
  local copies, waits for them, and re-layouts  3.95 us (3%)
    pallas_call x1, Pallas kernels, on_device(): pl.pallas_call(functools.partial(kernel, n_row), out_shape=jax.ShapeDtype...  140 us
    broadcast_in_dim x1, local copies, waits for them, and re-layouts, on_device(): return result[:, None, :]  3.27 us

profile of v1, /device:TPU:1, one launch (start us, length us, event | category | flops | bytes accessed | tf_op | source)
XLA Modules:
  0.0 144.9 jit_solution(8367441365713229903)
XLA Ops:
  0.0 0.0 copy-start
  0.0 0.7 copy-done
  0.7 0.2 select_reduce_fusion
  0.9 0.6 pad_add_fusion.table
  1.5 140.1 %shard_map.28 = f32[512,512]{1,0:T(8,128)} custom-call(s32[3,8]{1,0:T(4,128)} %pad_add_fusion.table, f32[16,1,16384]{2,1,0:T(1,128)} %snap.1), custom_call_target="tpu_custom_call" | custom-call | tf_op jit(solution)/shard_map/pallas_call | solution.py:233
  141.6 3.3 %copy.4 = f32[512,1,512]{2,1,0:T(1,128)} copy(f32[512,1,512]{2,0,1:T(8,128)} %bitcast.1) | data formatting | bytes 2097152 | tf_op jit(solution)/shard_map/broadcast_in_dim | solution.py:252
  (3 shorter events, 0.0 us)
Async XLA Ops:
  0.0 0.7 copy-start

commit v2 on v1

--- a/solution.py
+++ b/solution.py
@@ -14,12 +14,17 @@
 NT = (((1,), (1,)), ((), ()))
 TILES = [(i, j) for i in range(4) for j in range(i, 4)]
 TILE_ROWS = 128 * len(TILES)
+PIECES = (16, 16, 8)
 T2_AT, T4_AT, T8_AT = 49.0, 4801.0, 46099201.0
 INVERSE_SCALE = 32.0 * 5.0 * T2_AT * T4_AT / T8_AT
 
 
 def dot(left, right, dims=NN):
     return lax.dot_general(left, right, dims, preferred_element_type=F32)
+
+
+def chunk(at, size):
+    return pl.ds(pl.multiple_of(size * at, size), size)
 
 
 def split(value):
@@ -41,7 +46,7 @@
     return lax.broadcasted_iota(jnp.int32, shape, 0) == lax.broadcasted_iota(jnp.int32, shape, 1)
 
 
-def kernel(n_row, table, snap, out, S0, S1, S2, E, RSB, RED, G, f0, f1, h0, l0, h1, l1, h2, l2, h3,
+def kernel(n_row, plan, snap, out, S0, S1, S2, E, RSB, G0, G1, G2, T, f0, f1, h0, l0, h1, l1, h2, l2, h3,
            sem_in, sem_in_s, sem_sw, sem_sw_s, sem_rs, sem_rs_s, sem_ag, sem_ag_s):
     r = lax.axis_index("row")
     p = lax.axis_index("pair")
@@ -52,19 +57,26 @@
     order = 512
     half = 256
     S = (S0, S1, S2)
+    G = (G0, G1, G2)
     width = S0.shape[2]
     own = snap.shape[0]
     partner = (r, 2 * h + 1 - c)
 
+    zl, x, y = r // 16, lax.rem(r // 4, 4), lax.rem(r, 4)
+    z = 2 * h + zl
+
+    def device(dx, dy, dz):
+        px, py, pz = lax.rem(x + dx, 4), lax.rem(y + dy, 4), lax.rem(z + dz, 4)
+        return 16 * lax.rem(pz, 2) + 4 * px + py, 2 * (pz // 2) + c
+
     def peer_of(k):
-        peer = lax.rem(me + k, n_peer)
-        return lax.rem(peer, n_row), peer // n_row
+        k = lax.rem(37 * k, n_peer)
+        return device(lax.rem(k // 4, 4), lax.rem(k, 4), k // 16)
 
     barrier = pltpu.get_barrier_semaphore()
 
     def greet(k, carry):
-        pr, ph = peer_of(k)
-        pl.semaphore_signal(barrier, inc=1, device_id=(pr, 2 * ph + c), device_id_type=MESH)
+        pl.semaphore_signal(barrier, inc=1, device_id=peer_of(k), device_id_type=MESH)
         return carry
 
     pl.semaphore_signal(barrier, inc=1, device_id=partner, device_id_type=MESH)
@@ -77,12 +89,12 @@
     local.start()
 
     def scatter(k, carry):
-        pr, ph = peer_of(k)
+        pr, pp = peer_of(k)
         pltpu.make_async_remote_copy(
             src_ref=snap.at[:, 0, pl.ds(pl.multiple_of(width * pr, width), width)],
             dst_ref=mine,
             send_sem=sem_in_s, recv_sem=sem_in.at[h],
-            device_id=(pr, 2 * ph + c), device_id_type=MESH).start()
+            device_id=(pr, pp), device_id_type=MESH).start()
         return carry
 
     lax.fori_loop(1, n_peer, scatter, 0)
@@ -114,8 +126,15 @@
 
     eye = identity(order)
 
+    def place(round_at, block):
+        at = jnp.int32(0)
+        for k in range(1, 8):
+            at = at + k * (plan[round_at, k] == block).astype(jnp.int32)
+        return jnp.minimum(at, 7)
+
     def load_pair(s, q):
-        parts = [S[s][table[s, 2 * q + side]] for side in range(2)]
+        wanted = [plan[s, 2 * q + side] for side in range(2)]
+        parts = [S[s][block if s == 0 else place(0, block)] for block in wanted]
         return split(jnp.concatenate(parts, axis=0))
 
     def one_round(s):
@@ -129,7 +148,8 @@
             return pl.ds(pl.multiple_of(part * k, part), part)
 
         def reduce_send(k, c2):
-            pr = lax.rem(r + k, n_row)
+            k = lax.rem(21 * k, n_row)
+            pr = 16 * lax.rem(zl + k // 16, 2) + 4 * lax.rem(x + k // 4, 4) + lax.rem(y + k, 4)
             pltpu.make_async_remote_copy(
                 src_ref=E.at[s, slice_of(pr), :], dst_ref=RSB.at[s, slice_of(r), :],
                 send_sem=sem_rs_s.at[s], recv_sem=sem_rs.at[s],
@@ -142,24 +162,48 @@
         total = jnp.zeros((part, 128), F32)
         for k in range(n_row):
             total = total + RSB[s, pl.ds(part * k, part), :]
-        RED[s] = total
+        own_at = (16 * x + 4 * z + y, 16 * y + 4 * z + x, 16 * z + 4 * x + y)
+        line_at = (x, y, z)
+        first = 0
+        for colour, size in enumerate(PIECES):
+            G[colour][s, chunk(own_at[colour], size), :] = total[first:first + size]
+            first += size
+
+        def plane_send(k, c2):
+            k = lax.rem(7 * k, 16)
+            near, far = lax.rem(k, 4), k // 4
+            targets = (device(0, near, far), device(near, 0, far), device(far, near, 0))
+            for colour, size in enumerate(PIECES):
+                piece = G[colour].at[s, chunk(own_at[colour], size), :]
+                pltpu.make_async_remote_copy(
+                    src_ref=piece, dst_ref=piece,
+                    send_sem=sem_ag_s.at[s, colour, 0], recv_sem=sem_ag.at[s, colour, 0],
+                    device_id=targets[colour], device_id_type=MESH).start()
+            return c2
+
+        lax.fori_loop(1, 16, plane_send, 0)
         await_bytes(E.at[s, pl.ds(0, part * (n_row - 1)), :], sem_rs_s.at[s])
-
-        def gather_send(k, c2):
-            pr, ph = peer_of(k)
-            pltpu.make_async_remote_copy(
-                src_ref=RED.at[s], dst_ref=G.at[s, slice_of(h * n_row + r), :],
-                send_sem=sem_ag_s.at[s], recv_sem=sem_ag.at[s, h],
-                device_id=(pr, 2 * ph + c), device_id_type=MESH).start()
-            return c2
-
-        pltpu.make_async_copy(RED.at[s], G.at[s, slice_of(h * n_row + r), :], sem_ag.at[s, h]).start()
-        lax.fori_loop(1, n_peer, gather_send, 0)
+        for colour, size in enumerate(PIECES):
+            await_bytes(G[colour].at[s, pl.ds(0, 15 * size), :], sem_ag.at[s, colour, 0])
+            line = G[colour].at[s, chunk(line_at[colour], 16 * size), :]
+            for k in (2, 1, 3):
+                pltpu.make_async_remote_copy(
+                    src_ref=line, dst_ref=line,
+                    send_sem=sem_ag_s.at[s, colour, 1], recv_sem=sem_ag.at[s, colour, 1],
+                    device_id=(device(k, 0, 0), device(0, k, 0), device(0, 0, k))[colour],
+                    device_id_type=MESH).start()
+        for colour, size in enumerate(PIECES):
+            await_bytes(G[colour].at[s, pl.ds(0, 48 * size), :], sem_ag.at[s, colour, 1])
 
         def rotate(hq, c2):
-            base = pl.multiple_of(TILE_ROWS * hq, TILE_ROWS)
-            await_bytes(G.at[s, pl.ds(base, TILE_ROWS), :], sem_ag.at[s, hq])
-            tile = {ij: G[s, pl.ds(base + 128 * n, 128), :] for n, ij in enumerate(TILES)}
+            for k in range(n_row):
+                kz, kx, ky = 2 * hq + k // 16, (k // 4) % 4, k % 4
+                first = part * k
+                for colour, size in enumerate(PIECES):
+                    at = (16 * kx + 4 * kz + ky, 16 * ky + 4 * kz + kx, 16 * kz + 4 * kx + ky)[colour]
+                    T[pl.ds(first, size), :] = G[colour][s, chunk(at, size), :]
+                    first += size
+            tile = {ij: T[pl.ds(128 * n, 128), :] for n, ij in enumerate(TILES)}
             on = identity(128)
             columns, rows = [], []
             for i in range(4):
@@ -208,26 +252,19 @@
             return c2
 
         lax.fori_loop(0, 2, rotate, 0)
-        await_bytes(G.at[s, pl.ds(0, part * (n_peer - 1)), :], sem_ag_s.at[s])
+        for colour, size in enumerate(PIECES):
+            await_bytes(G[colour].at[s, pl.ds(0, 15 * size), :], sem_ag_s.at[s, colour, 0])
+            await_bytes(G[colour].at[s, pl.ds(0, 48 * size), :], sem_ag_s.at[s, colour, 1])
         await_swap(s + 1)
 
     one_round(0)
     one_round(1)
     for side in range(2):
-        out[pl.ds(half * side, half), :] = S2[table[2, 2 * p + side]]
-
-
-def places(plan):
-    natural = jnp.arange(plan.shape[1], dtype=jnp.int32)
-    wanted = jnp.stack([plan[1], natural])
-    hits = plan[:, None, :] == wanted[:, :, None]
-    found = jnp.sum(jnp.where(hits, natural, 0), axis=2)
-    return jnp.concatenate([plan[:1], found], axis=0)
+        out[pl.ds(half * side, half), :] = S2[place(1, 2 * p + side)]
 
 
 def on_device(n_row, snapshots, plan):
     width = snapshots.shape[2] // n_row
-    part = TILE_ROWS // n_row
     dma = pltpu.SemaphoreType.DMA
     full = (512, 512)
     result = pl.pallas_call(
@@ -239,16 +276,16 @@
             pltpu.VMEM((8, 256, width), F32), pltpu.VMEM((8, 256, width), F32), pltpu.VMEM((8, 256, width), F32),
             pltpu.VMEM((2, TILE_ROWS, 128), F32),
             pltpu.VMEM((2, TILE_ROWS, 128), F32),
-            pltpu.VMEM((2, part, 128), F32),
-            pltpu.VMEM((2, 2 * TILE_ROWS, 128), F32),
+            *[pltpu.VMEM((2, 64 * size, 128), F32) for size in PIECES],
+            pltpu.VMEM((TILE_ROWS, 128), F32),
             pltpu.VMEM(full, F32), pltpu.VMEM(full, F32),
             pltpu.VMEM(full, BF16), pltpu.VMEM(full, BF16), pltpu.VMEM(full, BF16), pltpu.VMEM(full, BF16),
             pltpu.VMEM(full, BF16), pltpu.VMEM(full, BF16), pltpu.VMEM(full, BF16),
-            dma((2,)), dma, dma((3, 2)), dma((3, 2)), dma((2,)), dma((2,)), dma((2, 2)), dma((2,)),
+            dma((2,)), dma, dma((3, 2)), dma((3, 2)), dma((2,)), dma((2,)), dma((2, 3, 2)), dma((2, 3, 2)),
         ],
         compiler_params=pltpu.CompilerParams(
             collective_id=0, has_side_effects=True, vmem_limit_bytes=60 * 1024 * 1024),
-    )(places(plan), snapshots)
+    )(plan, snapshots)
     return result[:, None, :]
 
 

time: 145 us -> 124 us (0.86)
  Pallas kernels: 140 us -> 121 us
    pallas_call x1, Pallas kernels: 140 us -> 121 us  [on_device(): pl.pallas_call(functools.partial(kernel, n_row), out_shape=jax.ShapeDtype...]
where the time goes in v2:
time: 124 us
  Pallas kernels  121 us (98%)
  local copies, waits for them, and re-layouts  3.27 us (3%)
    pallas_call x1, Pallas kernels, on_device(): pl.pallas_call(functools.partial(kernel, n_row), out_shape=jax.ShapeDtype...  121 us
    broadcast_in_dim x1, local copies, waits for them, and re-layouts, on_device(): return result[:, None, :]  3.27 us

profile of v2, /device:TPU:1, one launch (start us, length us, event | category | flops | bytes accessed | tf_op | source)
XLA Modules:
  0.0 123.8 jit_solution(13095795860780268812)
XLA Ops:
  0.0 120.5 %shard_map.28 = f32[512,512]{1,0:T(8,128)} custom-call(s32[2,8]{1,0:T(2,128)} %plan.1, f32[16,1,16384]{2,1,0:T(1,128)} %snap.1), custom_call_target="tpu_custom_call" | custom-call | tf_op jit(solution)/shard_map/pallas_call | solution.py:270
  120.5 3.3 %copy.3 = f32[512,1,512]{2,1,0:T(1,128)} copy(f32[512,1,512]{2,0,1:T(8,128)} %bitcast.1) | data formatting | bytes 2097152 | tf_op jit(solution)/shard_map/broadcast_in_dim | solution.py:289

commit v3 on v2

--- a/solution.py
+++ b/solution.py
@@ -15,8 +15,6 @@
 TILES = [(i, j) for i in range(4) for j in range(i, 4)]
 TILE_ROWS = 128 * len(TILES)
 PIECES = (16, 16, 8)
-T2_AT, T4_AT, T8_AT = 49.0, 4801.0, 46099201.0
-INVERSE_SCALE = 32.0 * 5.0 * T2_AT * T4_AT / T8_AT
 
 
 def dot(left, right, dims=NN):
@@ -46,8 +44,8 @@
     return lax.broadcasted_iota(jnp.int32, shape, 0) == lax.broadcasted_iota(jnp.int32, shape, 1)
 
 
-def kernel(n_row, plan, snap, out, S0, S1, S2, E, RSB, G0, G1, G2, T, f0, f1, h0, l0, h1, l1, h2, l2, h3,
-           sem_in, sem_in_s, sem_sw, sem_sw_s, sem_rs, sem_rs_s, sem_ag, sem_ag_s):
+def kernel(n_row, plan, snap, out, S0, S1, S2, E, B0, B1, B2, G0, G1, G2, T, f0, f1, h0, l0, h1, l1, h2, h3,
+           sem_in, sem_in_s, sem_fw, sem_fw_s, sem_sw, sem_sw_s, sem_rs, sem_rs_s, sem_ag, sem_ag_s):
     r = lax.axis_index("row")
     p = lax.axis_index("pair")
     h, c = p // 2, p % 2
@@ -58,6 +56,7 @@
     half = 256
     S = (S0, S1, S2)
     G = (G0, G1, G2)
+    RSB = (B0, B1, B2)
     width = S0.shape[2]
     own = snap.shape[0]
     partner = (r, 2 * h + 1 - c)
@@ -73,6 +72,10 @@
         k = lax.rem(37 * k, n_peer)
         return device(lax.rem(k // 4, 4), lax.rem(k, 4), k // 16)
 
+    def source_of(k):
+        k = lax.rem(37 * k, n_peer)
+        return device(lax.rem(4 - k // 4 % 4, 4), lax.rem(4 - k % 4, 4), lax.rem(4 - k // 16, 4))
+
     barrier = pltpu.get_barrier_semaphore()
 
     def greet(k, carry):
@@ -83,21 +86,41 @@
     lax.fori_loop(1, n_peer, greet, 0)
     pl.semaphore_wait(barrier, n_peer)
 
-    mine = S0.at[2 * p + (own * r) // half, pl.ds(pl.multiple_of(lax.rem(own * r, half), own), own), :]
-    local = pltpu.make_async_copy(
-        snap.at[:, 0, pl.ds(pl.multiple_of(width * r, width), width)], mine, sem_in.at[h])
+    def home(row_at, pair_at):
+        first = own * row_at
+        return S0.at[2 * pair_at + first // half, pl.ds(pl.multiple_of(lax.rem(first, half), own), own), :]
+
+    def columns_for(row_at):
+        return snap.at[:, 0, pl.ds(pl.multiple_of(width * row_at, width), width)]
+
+    local = pltpu.make_async_copy(columns_for(r), home(r, p), sem_in.at[0])
     local.start()
 
     def scatter(k, carry):
         pr, pp = peer_of(k)
         pltpu.make_async_remote_copy(
-            src_ref=snap.at[:, 0, pl.ds(pl.multiple_of(width * pr, width), width)],
-            dst_ref=mine,
-            send_sem=sem_in_s, recv_sem=sem_in.at[h],
+            src_ref=columns_for(pr), dst_ref=home(r, p),
+            send_sem=sem_in_s, recv_sem=sem_in.at[k],
             device_id=(pr, pp), device_id_type=MESH).start()
         return carry
 
     lax.fori_loop(1, n_peer, scatter, 0)
+
+    def forward(k, carry):
+        arrived = home(*source_of(k))
+        await_bytes(arrived, sem_in.at[k])
+        pltpu.make_async_remote_copy(
+            src_ref=arrived, dst_ref=arrived, send_sem=sem_fw_s, recv_sem=sem_fw,
+            device_id=partner, device_id_type=MESH).start()
+        return carry
+
+    def await_bytes(ref, sem):
+        pltpu.make_async_copy(ref, ref, sem).wait()
+
+    lax.fori_loop(0, n_peer, forward, 0)
+    await_bytes(S0.at[pl.ds(0, 6), pl.ds(0, own * (n_peer - 1) // 6), :], sem_in_s)
+    await_bytes(S0.at[pl.ds(0, 4)], sem_fw)
+    await_bytes(S0.at[pl.ds(0, 4)], sem_fw_s)
 
     def blocks_of(s, q):
         return S[s].at[pl.ds(2 * q, 2)]
@@ -106,23 +129,14 @@
         q = 2 * hq + c
         return pltpu.make_async_remote_copy(
             src_ref=blocks_of(s, q), dst_ref=blocks_of(s, q),
-            send_sem=sem_sw_s.at[s, hq], recv_sem=sem_sw.at[s, hq],
+            send_sem=sem_sw_s.at[s - 1, hq], recv_sem=sem_sw.at[s - 1, hq],
             device_id=partner, device_id_type=MESH)
-
-    def await_bytes(ref, sem):
-        pltpu.make_async_copy(ref, ref, sem).wait()
 
     def await_swap(s):
         for hq in range(2):
             other = blocks_of(s, 2 * hq + 1 - c)
-            await_bytes(other, sem_sw.at[s, hq])
-            await_bytes(other, sem_sw_s.at[s, hq])
-
-    for hq in range(2):
-        await_bytes(blocks_of(0, 2 * hq + c), sem_in.at[hq])
-        swap(0, hq).start()
-    await_bytes(S0.at[pl.ds(0, 6), pl.ds(0, own * (n_peer - 1) // 6), :], sem_in_s)
-    await_swap(0)
+            await_bytes(other, sem_sw.at[s - 1, hq])
+            await_bytes(other, sem_sw_s.at[s - 1, hq])
 
     eye = identity(order)
 
@@ -144,45 +158,46 @@
         for n, (i, j) in enumerate(TILES):
             E[s, pl.ds(128 * n, 128), :] = gram[128 * i:128 * i + 128, 128 * j:128 * j + 128]
 
-        def slice_of(k):
-            return pl.ds(pl.multiple_of(part * k, part), part)
-
-        def reduce_send(k, c2):
-            k = lax.rem(21 * k, n_row)
-            pr = 16 * lax.rem(zl + k // 16, 2) + 4 * lax.rem(x + k // 4, 4) + lax.rem(y + k, 4)
-            pltpu.make_async_remote_copy(
-                src_ref=E.at[s, slice_of(pr), :], dst_ref=RSB.at[s, slice_of(r), :],
-                send_sem=sem_rs_s.at[s], recv_sem=sem_rs.at[s],
-                device_id=(pr, p), device_id_type=MESH).start()
-            return c2
-
-        pltpu.make_async_copy(E.at[s, slice_of(r), :], RSB.at[s, slice_of(r), :], sem_rs.at[s]).start()
-        lax.fori_loop(1, n_row, reduce_send, 0)
-        await_bytes(RSB.at[s], sem_rs.at[s])
-        total = jnp.zeros((part, 128), F32)
-        for k in range(n_row):
-            total = total + RSB[s, pl.ds(part * k, part), :]
         own_at = (16 * x + 4 * z + y, 16 * y + 4 * z + x, 16 * z + 4 * x + y)
         line_at = (x, y, z)
-        first = 0
-        for colour, size in enumerate(PIECES):
-            G[colour][s, chunk(own_at[colour], size), :] = total[first:first + size]
-            first += size
-
-        def plane_send(k, c2):
-            k = lax.rem(7 * k, 16)
-            near, far = lax.rem(k, 4), k // 4
-            targets = (device(0, near, far), device(near, 0, far), device(far, near, 0))
-            for colour, size in enumerate(PIECES):
+
+        def piece_of(colour, k):
+            first = part * k + sum(PIECES[:colour])
+            return E.at[s, pl.ds(pl.multiple_of(first, 8), PIECES[colour]), :]
+
+        for colour, size in enumerate(PIECES):
+            def reduce_send(k, c2):
+                k = lax.rem(21 * k, n_row)
+                pr = 16 * lax.rem(zl + k // 16, 2) + 4 * lax.rem(x + k // 4, 4) + lax.rem(y + k, 4)
+                pltpu.make_async_remote_copy(
+                    src_ref=piece_of(colour, pr), dst_ref=RSB[colour].at[s, chunk(r, size), :],
+                    send_sem=sem_rs_s.at[s, colour], recv_sem=sem_rs.at[s, colour],
+                    device_id=(pr, p), device_id_type=MESH).start()
+                return c2
+
+            pltpu.make_async_copy(
+                piece_of(colour, r), RSB[colour].at[s, chunk(r, size), :], sem_rs.at[s, colour]).start()
+            lax.fori_loop(1, n_row, reduce_send, 0)
+
+        for colour, size in enumerate(PIECES):
+            await_bytes(RSB[colour].at[s], sem_rs.at[s, colour])
+            total = jnp.zeros((size, 128), F32)
+            for k in range(n_row):
+                total = total + RSB[colour][s, pl.ds(size * k, size), :]
+            G[colour][s, chunk(own_at[colour], size), :] = total
+
+            def plane_send(k, c2):
+                k = lax.rem(7 * k, 16)
+                near, far = lax.rem(k, 4), k // 4
+                target = (device(0, near, far), device(near, 0, far), device(far, near, 0))[colour]
                 piece = G[colour].at[s, chunk(own_at[colour], size), :]
                 pltpu.make_async_remote_copy(
                     src_ref=piece, dst_ref=piece,
                     send_sem=sem_ag_s.at[s, colour, 0], recv_sem=sem_ag.at[s, colour, 0],
-                    device_id=targets[colour], device_id_type=MESH).start()
-            return c2
-
-        lax.fori_loop(1, 16, plane_send, 0)
-        await_bytes(E.at[s, pl.ds(0, part * (n_row - 1)), :], sem_rs_s.at[s])
+                    device_id=target, device_id_type=MESH).start()
+                return c2
+
+            lax.fori_loop(1, 16, plane_send, 0)
         for colour, size in enumerate(PIECES):
             await_bytes(G[colour].at[s, pl.ds(0, 15 * size), :], sem_ag.at[s, colour, 0])
             line = G[colour].at[s, chunk(line_at[colour], 16 * size), :]
@@ -230,19 +245,21 @@
                 if i != j:
                     f0[pl.ds(128 * j, 128), pl.ds(128 * i, 128)] = -scaled.T
             h0[...], l0[...] = split(f0[...])
-            a = (h0[...], l0[...])
-            f1[...] = 4.0 * dot3(a, a) + jnp.where(eye, 1.0, 0.0)
-            h1[...], l1[...] = split(f1[...])
-            w = (h1[...], l1[...])
-            h2[...], l2[...] = split(2.0 * dot3(w, w) - jnp.where(eye, 1.0, 0.0))
-            t2 = (h2[...], l2[...])
-            h3[...] = (2.0 * dot(h2[...], h2[...]) - jnp.where(eye, 1.0, 0.0)).astype(BF16)
-            f0[...] = jnp.where(eye, 1.0, 0.0) - f0[...] + 0.2 * (f1[...] - dot3(a, w))
-            h0[...], l0[...] = split(f0[...])
-            f0[...] = f0[...] + (1.0 / T2_AT) * dot3((h0[...], l0[...]), t2)
+            square = dot(h0[...], h0[...])
+            h1[...] = square.astype(BF16)
+            f1[...] = (32.0 / 49.0) * square - (48.0 / 49.0) * f0[...] + jnp.where(eye, 48.0 / 49.0, 0.0)
+            h2[...] = (f1[...] - (32.0 / 49.0) * dot(h0[...], h1[...])).astype(BF16)
+            f0[...] = (
+                jnp.where(eye, 1.0, 0.0) - h2[...].astype(F32) - (dot(h0[...], h2[...]) + dot(l0[...], h2[...])))
+            h1[...] = f0[...].astype(BF16)
+            square = dot(h1[...], h1[...])
+            h3[...] = square.astype(BF16)
+            h0[...], l0[...] = split(f0[...] + square)
+            f0[...] = h2[...].astype(F32) + (dot(h2[...], h0[...]) + dot(h2[...], l0[...]))
+            h2[...] = dot(h1[...], h3[...]).astype(BF16)
             h0[...] = f0[...].astype(BF16)
-            f0[...] = f0[...] + (1.0 / T4_AT) * dot(h0[...], h3[...])
-            h0[...], l0[...] = split((2.0 * INVERSE_SCALE) * f0[...] - jnp.where(eye, 1.0, 0.0))
+            inverse = f0[...] + dot(h0[...], h2[...])
+            h0[...], l0[...] = split(2.0 * inverse - jnp.where(eye, 1.0, 0.0))
             q = 2 * hq + c
             h1[...], l1[...] = load_pair(s, q)
             turned = dot3((h0[...], l0[...]), (h1[...], l1[...]))
@@ -253,6 +270,7 @@
 
         lax.fori_loop(0, 2, rotate, 0)
         for colour, size in enumerate(PIECES):
+            await_bytes(RSB[colour].at[s, pl.ds(0, size * (n_row - 1)), :], sem_rs_s.at[s, colour])
             await_bytes(G[colour].at[s, pl.ds(0, 15 * size), :], sem_ag_s.at[s, colour, 0])
             await_bytes(G[colour].at[s, pl.ds(0, 48 * size), :], sem_ag_s.at[s, colour, 1])
         await_swap(s + 1)
@@ -275,13 +293,13 @@
         scratch_shapes=[
             pltpu.VMEM((8, 256, width), F32), pltpu.VMEM((8, 256, width), F32), pltpu.VMEM((8, 256, width), F32),
             pltpu.VMEM((2, TILE_ROWS, 128), F32),
-            pltpu.VMEM((2, TILE_ROWS, 128), F32),
+            *[pltpu.VMEM((2, n_row * size, 128), F32) for size in PIECES],
             *[pltpu.VMEM((2, 64 * size, 128), F32) for size in PIECES],
             pltpu.VMEM((TILE_ROWS, 128), F32),
             pltpu.VMEM(full, F32), pltpu.VMEM(full, F32),
             pltpu.VMEM(full, BF16), pltpu.VMEM(full, BF16), pltpu.VMEM(full, BF16), pltpu.VMEM(full, BF16),
-            pltpu.VMEM(full, BF16), pltpu.VMEM(full, BF16), pltpu.VMEM(full, BF16),
-            dma((2,)), dma, dma((3, 2)), dma((3, 2)), dma((2,)), dma((2,)), dma((2, 3, 2)), dma((2, 3, 2)),
+            pltpu.VMEM(full, BF16), pltpu.VMEM(full, BF16),
+            dma((2 * n_row,)), dma, dma, dma, dma((2, 2)), dma((2, 2)), dma((2, 3)), dma((2, 3)), dma((2, 3, 2)), dma((2, 3, 2)),
         ],
         compiler_params=pltpu.CompilerParams(
             collective_id=0, has_side_effects=True, vmem_limit_bytes=60 * 1024 * 1024),

time: 124 us -> 114 us (0.919)
  Pallas kernels: 121 us -> 110 us
    pallas_call x1, Pallas kernels: 121 us -> 110 us  [on_device(): pl.pallas_call(functools.partial(kernel, n_row), out_shape=jax.ShapeDtype...]
where the time goes in v3:
time: 114 us; the launch traced here: 113 us
  Pallas kernels  110 us (96%)
  local copies, waits for them, and re-layouts  3.27 us (3%)
    pallas_call x1, Pallas kernels, on_device(): pl.pallas_call(functools.partial(kernel, n_row), out_shape=jax.ShapeDtype...  110 us
    broadcast_in_dim x1, local copies, waits for them, and re-layouts, on_device(): return result[:, None, :]  3.27 us

profile of v3, /device:TPU:1, one launch (start us, length us, event | category | flops | bytes accessed | tf_op | source)
XLA Modules:
  0.0 113.0 jit_solution(6392452742137736933)
XLA Ops:
  0.0 109.7 %shard_map.28 = f32[512,512]{1,0:T(8,128)} custom-call(s32[2,8]{1,0:T(2,128)} %plan.1, f32[16,1,16384]{2,1,0:T(1,128)} %snap.1), custom_call_target="tpu_custom_call" | custom-call | tf_op jit(solution)/shard_map/pallas_call | solution.py:288
  109.7 3.3 %copy.3 = f32[512,1,512]{2,1,0:T(1,128)} copy(f32[512,1,512]{2,0,1:T(8,128)} %bitcast.1) | data formatting | bytes 2097152 | tf_op jit(solution)/shard_map/broadcast_in_dim | solution.py:307

commit v4 on v3

--- a/solution.py
+++ b/solution.py
@@ -12,9 +12,10 @@
 BF16 = jnp.bfloat16
 NN = (((1,), (0,)), ((), ()))
 NT = (((1,), (1,)), ((), ()))
-TILES = [(i, j) for i in range(4) for j in range(i, 4)]
+TILES = [(i, j) for i in range(4) for j in range(i + 1, 4)] + [(0, 0), (2, 2)]
 TILE_ROWS = 128 * len(TILES)
-PIECES = (16, 16, 8)
+PIECES = (8, 8, 16)
+ORDER = [(2, PIECES[2]), (0, PIECES[0]), (1, PIECES[1])]
 
 
 def dot(left, right, dims=NN):
@@ -44,8 +45,8 @@
     return lax.broadcasted_iota(jnp.int32, shape, 0) == lax.broadcasted_iota(jnp.int32, shape, 1)
 
 
-def kernel(n_row, plan, snap, out, S0, S1, S2, E, B0, B1, B2, G0, G1, G2, T, f0, f1, h0, l0, h1, l1, h2, h3,
-           sem_in, sem_in_s, sem_fw, sem_fw_s, sem_sw, sem_sw_s, sem_rs, sem_rs_s, sem_ag, sem_ag_s):
+def kernel(n_row, plan, snap, out, S0, S1, S2, E, B0, B1, B2, G0, G1, G2, T, D, DB, DS, f0, f1, h0, l0, h1, l1, h2, h3,
+           sem_d, sem_d_s, sem_ds, sem_ds_s, sem_in, sem_in_s, sem_fw, sem_fw_s, sem_sw, sem_sw_s, sem_rs, sem_rs_s, sem_ag, sem_ag_s):
     r = lax.axis_index("row")
     p = lax.axis_index("pair")
     h, c = p // 2, p % 2
@@ -139,6 +140,10 @@
             await_bytes(other, sem_sw_s.at[s - 1, hq])
 
     eye = identity(order)
+    on = identity(128)
+    row_ids = lax.broadcasted_iota(jnp.int32, (128, 128), 0)
+    column_ids = lax.broadcasted_iota(jnp.int32, (128, 128), 1)
+    D[...] = jnp.zeros_like(D)
 
     def place(round_at, block):
         at = jnp.int32(0)
@@ -151,12 +156,53 @@
         parts = [S[s][block if s == 0 else place(0, block)] for block in wanted]
         return split(jnp.concatenate(parts, axis=0))
 
+    def send_diagonal(s):
+        @pl.when(r > 0)
+        def _():
+            pltpu.make_async_remote_copy(
+                src_ref=D.at[s], dst_ref=DB.at[s, r], send_sem=sem_d_s.at[s], recv_sem=sem_d.at[s],
+                device_id=(0, p), device_id_type=MESH).start()
+
+    def sum_diagonal(s):
+        @pl.when(r == 0)
+        def _():
+            await_bytes(DB.at[s, pl.ds(1, n_row - 1)], sem_d.at[s])
+            total = D[s]
+            for k in range(1, n_row):
+                total = total + DB[s, k]
+            DS[s, h] = total
+
+            def send(k, carry):
+                pltpu.make_async_remote_copy(
+                    src_ref=DS.at[s, h], dst_ref=DS.at[s, h], send_sem=sem_ds_s.at[s], recv_sem=sem_ds.at[s, h],
+                    device_id=peer_of(k), device_id_type=MESH).start()
+                return carry
+
+            lax.fori_loop(1, n_peer, send, 0)
+
+    def await_diagonal(s):
+        @pl.when(r > 0)
+        def _():
+            await_bytes(D.at[s], sem_d_s.at[s])
+            await_bytes(DS.at[s, h], sem_ds.at[s, h])
+
+        await_bytes(DS.at[s, 1 - h], sem_ds.at[s, 1 - h])
+
+        @pl.when(r == 0)
+        def _():
+            await_bytes(T.at[pl.ds(0, 8 * (n_peer - 1)), :], sem_ds_s.at[s])
+
     def one_round(s):
         h0[...], l0[...] = load_pair(s, p)
         pair = (h0[...], l0[...])
         gram = dot3(pair, pair, NT)
         for n, (i, j) in enumerate(TILES):
-            E[s, pl.ds(128 * n, 128), :] = gram[128 * i:128 * i + 128, 128 * j:128 * j + 128]
+            tile = gram[128 * i:128 * i + 128, 128 * j:128 * j + 128]
+            if i == j:
+                second = gram[128 * i + 128:128 * i + 256, 128 * i + 128:128 * i + 256]
+                tile = jnp.where(column_ids >= row_ids, tile, second)
+                D[s, i // 2:i // 2 + 1, :] = jnp.sum(jnp.where(on, second, 0.0), axis=0, keepdims=True)
+            E[s, pl.ds(128 * n, 128), :] = tile
 
         own_at = (16 * x + 4 * z + y, 16 * y + 4 * z + x, 16 * z + 4 * x + y)
         line_at = (x, y, z)
@@ -165,7 +211,8 @@
             first = part * k + sum(PIECES[:colour])
             return E.at[s, pl.ds(pl.multiple_of(first, 8), PIECES[colour]), :]
 
-        for colour, size in enumerate(PIECES):
+        send_diagonal(s)
+        for colour, size in ORDER:
             def reduce_send(k, c2):
                 k = lax.rem(21 * k, n_row)
                 pr = 16 * lax.rem(zl + k // 16, 2) + 4 * lax.rem(x + k // 4, 4) + lax.rem(y + k, 4)
@@ -179,7 +226,7 @@
                 piece_of(colour, r), RSB[colour].at[s, chunk(r, size), :], sem_rs.at[s, colour]).start()
             lax.fori_loop(1, n_row, reduce_send, 0)
 
-        for colour, size in enumerate(PIECES):
+        for colour, size in ORDER:
             await_bytes(RSB[colour].at[s], sem_rs.at[s, colour])
             total = jnp.zeros((size, 128), F32)
             for k in range(n_row):
@@ -198,7 +245,8 @@
                 return c2
 
             lax.fori_loop(1, 16, plane_send, 0)
-        for colour, size in enumerate(PIECES):
+        sum_diagonal(s)
+        for colour, size in ORDER:
             await_bytes(G[colour].at[s, pl.ds(0, 15 * size), :], sem_ag.at[s, colour, 0])
             line = G[colour].at[s, chunk(line_at[colour], 16 * size), :]
             for k in (2, 1, 3):
@@ -207,8 +255,9 @@
                     send_sem=sem_ag_s.at[s, colour, 1], recv_sem=sem_ag.at[s, colour, 1],
                     device_id=(device(k, 0, 0), device(0, k, 0), device(0, 0, k))[colour],
                     device_id_type=MESH).start()
-        for colour, size in enumerate(PIECES):
+        for colour, size in ORDER:
             await_bytes(G[colour].at[s, pl.ds(0, 48 * size), :], sem_ag.at[s, colour, 1])
+        await_diagonal(s)
 
         def rotate(hq, c2):
             for k in range(n_row):
@@ -219,30 +268,32 @@
                     T[pl.ds(first, size), :] = G[colour][s, chunk(at, size), :]
                     first += size
             tile = {ij: T[pl.ds(128 * n, 128), :] for n, ij in enumerate(TILES)}
-            on = identity(128)
             columns, rows = [], []
             for i in range(4):
-                diagonal = jnp.where(on, tile[i, i], 0.0)
+                if i % 2 == 0:
+                    diagonal = jnp.where(on, tile[i, i], 0.0)
+                else:
+                    diagonal = jnp.where(on, DS[s, hq, i // 2:i // 2 + 1, :], 0.0)
                 columns.append(lax.rsqrt(jnp.sum(diagonal, axis=1, keepdims=True)))
                 rows.append(lax.rsqrt(jnp.sum(diagonal, axis=0, keepdims=True)))
-            row_ids = lax.broadcasted_iota(jnp.int32, (128, 128), 0)
-            column_ids = lax.broadcasted_iota(jnp.int32, (128, 128), 1)
-            signs = jnp.where(column_ids > row_ids, 1.0, jnp.where(column_ids < row_ids, -1.0, 0.0))
             squares = jnp.zeros((128, 128), F32)
             skew = {}
             for i, j in TILES:
                 normed = tile[i, j] * columns[i] * rows[j]
                 if i == j:
-                    normed = normed * signs
-                    squares = squares + normed * normed
+                    normed = jnp.where(column_ids > row_ids, normed, 0.0)
+                    other = tile[i, i] * columns[i + 1] * rows[i + 1]
+                    skew[i + 1, i + 1] = jnp.where(column_ids < row_ids, -other, 0.0)
+                    squares = squares + skew[i + 1, i + 1] * skew[i + 1, i + 1]
+                skew[i, j] = normed
+                squares = squares + normed * normed
+            scale = 1.0 / (1.0 + jnp.sqrt(2.0 * jnp.sum(squares, keepdims=True)))
+            for i, j in skew:
+                scaled = skew[i, j] * scale
+                if i == j:
+                    f0[pl.ds(128 * i, 128), pl.ds(128 * i, 128)] = scaled - scaled.T
                 else:
-                    squares = squares + 2.0 * (normed * normed)
-                skew[i, j] = normed
-            scale = 1.0 / (1.0 + jnp.sqrt(jnp.sum(squares, keepdims=True)))
-            for i, j in TILES:
-                scaled = skew[i, j] * scale
-                f0[pl.ds(128 * i, 128), pl.ds(128 * j, 128)] = scaled
-                if i != j:
+                    f0[pl.ds(128 * i, 128), pl.ds(128 * j, 128)] = scaled
                     f0[pl.ds(128 * j, 128), pl.ds(128 * i, 128)] = -scaled.T
             h0[...], l0[...] = split(f0[...])
             square = dot(h0[...], h0[...])
@@ -269,7 +320,7 @@
             return c2
 
         lax.fori_loop(0, 2, rotate, 0)
-        for colour, size in enumerate(PIECES):
+        for colour, size in ORDER:
             await_bytes(RSB[colour].at[s, pl.ds(0, size * (n_row - 1)), :], sem_rs_s.at[s, colour])
             await_bytes(G[colour].at[s, pl.ds(0, 15 * size), :], sem_ag_s.at[s, colour, 0])
             await_bytes(G[colour].at[s, pl.ds(0, 48 * size), :], sem_ag_s.at[s, colour, 1])
@@ -279,6 +330,12 @@
     one_round(1)
     for side in range(2):
         out[pl.ds(half * side, half), :] = S2[place(1, 2 * p + side)]
+
+
+def deliver(blocks, out, sem):
+    copy = pltpu.make_async_copy(blocks, out.at[:, 0, :], sem)
+    copy.start()
+    copy.wait()
 
 
 def on_device(n_row, snapshots, plan):
@@ -288,7 +345,7 @@
     result = pl.pallas_call(
         functools.partial(kernel, n_row),
         out_shape=jax.ShapeDtypeStruct((512, width), F32),
-        in_specs=[pl.BlockSpec(memory_space=pltpu.SMEM), pl.BlockSpec(memory_space=pl.ANY)],
+        in_specs=[pl.BlockSpec(memory_space=pltpu.SMEM), pl.BlockSpec(memory_space=pltpu.HBM)],
         out_specs=pl.BlockSpec(memory_space=pltpu.VMEM),
         scratch_shapes=[
             pltpu.VMEM((8, 256, width), F32), pltpu.VMEM((8, 256, width), F32), pltpu.VMEM((8, 256, width), F32),
@@ -296,15 +353,23 @@
             *[pltpu.VMEM((2, n_row * size, 128), F32) for size in PIECES],
             *[pltpu.VMEM((2, 64 * size, 128), F32) for size in PIECES],
             pltpu.VMEM((TILE_ROWS, 128), F32),
+            pltpu.VMEM((2, 8, 128), F32), pltpu.VMEM((2, n_row, 8, 128), F32), pltpu.VMEM((2, 2, 8, 128), F32),
             pltpu.VMEM(full, F32), pltpu.VMEM(full, F32),
             pltpu.VMEM(full, BF16), pltpu.VMEM(full, BF16), pltpu.VMEM(full, BF16), pltpu.VMEM(full, BF16),
             pltpu.VMEM(full, BF16), pltpu.VMEM(full, BF16),
-            dma((2 * n_row,)), dma, dma, dma, dma((2, 2)), dma((2, 2)), dma((2, 3)), dma((2, 3)), dma((2, 3, 2)), dma((2, 3, 2)),
+            dma((2,)), dma((2,)), dma((2, 2)), dma((2,)), dma((2 * n_row,)), dma, dma, dma, dma((2, 2)), dma((2, 2)), dma((2, 3)), dma((2, 3)), dma((2, 3, 2)), dma((2, 3, 2)),
         ],
         compiler_params=pltpu.CompilerParams(
-            collective_id=0, has_side_effects=True, vmem_limit_bytes=60 * 1024 * 1024),
-    )(plan, snapshots)
-    return result[:, None, :]
+            collective_id=0, has_side_effects=True, vmem_limit_bytes=32 * 1024 * 1024),
+    )(pltpu.with_memory_space_constraint(plan, pltpu.HBM), pltpu.with_memory_space_constraint(snapshots, pltpu.HBM))
+    return pl.pallas_call(
+        deliver,
+        out_shape=jax.ShapeDtypeStruct((512, 1, width), F32),
+        in_specs=[pl.BlockSpec(memory_space=pl.ANY)],
+        out_specs=pl.BlockSpec(memory_space=pltpu.HBM),
+        scratch_shapes=[dma],
+        compiler_params=pltpu.CompilerParams(vmem_limit_bytes=4 * 1024 * 1024),
+    )(result)
 
 
 def solution(mesh):

time: 114 us -> 106 us (0.930)
  Pallas kernels: 110 us -> 106 us
  local copies, waits for them, and re-layouts: 3.27 us -> 0 us
    pallas_call x1, Pallas kernels: 110 us -> 105 us  [on_device(): pl.pallas_call(functools.partial(kernel, n_row), out_shape=jax.ShapeDtype...]
    broadcast_in_dim x1 -> x0, local copies, waits for them, and re-layouts: 3.27 us -> none  [on_device(): return result[:, None, :]]
where the time goes in v4:
time: 106 us
  Pallas kernels  106 us (100%)
    pallas_call x1, Pallas kernels, on_device(): pl.pallas_call(functools.partial(kernel, n_row), out_shape=jax.ShapeDtype...  105 us

profile of v4, /device:TPU:1, one launch (start us, length us, event | category | flops | bytes accessed | tf_op | source)
XLA Modules:
  0.0 105.6 jit_solution(7630745127345942595)
XLA Ops:
  0.0 104.6 %shard_map.28.blocks = f32[512,512]{1,0:T(8,128)S(1)} custom-call(s32[2,8]{1,0:T(2,128)} %plan.1, f32[16,1,16384]{2,1,0:T(1,128)} %snap.1), custom_call_target="tpu_custom_call" | custom-call | tf_op jit(solution)/shard_map/pallas_call | solution.py:345
  104.6 1.0 shard_map.29

commit v5 on v4

--- a/solution.py
+++ b/solution.py
@@ -123,21 +123,19 @@
     await_bytes(S0.at[pl.ds(0, 4)], sem_fw)
     await_bytes(S0.at[pl.ds(0, 4)], sem_fw_s)
 
-    def blocks_of(s, q):
-        return S[s].at[pl.ds(2 * q, 2)]
-
-    def swap(s, hq):
-        q = 2 * hq + c
+    def swap(s, hq, side):
+        block = S[s].at[2 * (2 * hq + c) + side]
         return pltpu.make_async_remote_copy(
-            src_ref=blocks_of(s, q), dst_ref=blocks_of(s, q),
-            send_sem=sem_sw_s.at[s - 1, hq], recv_sem=sem_sw.at[s - 1, hq],
+            src_ref=block, dst_ref=block,
+            send_sem=sem_sw_s.at[s - 1, hq, side], recv_sem=sem_sw.at[s - 1, hq, side],
             device_id=partner, device_id_type=MESH)
 
     def await_swap(s):
         for hq in range(2):
-            other = blocks_of(s, 2 * hq + 1 - c)
-            await_bytes(other, sem_sw.at[s - 1, hq])
-            await_bytes(other, sem_sw_s.at[s - 1, hq])
+            for side in range(2):
+                other = S[s].at[2 * (2 * hq + 1 - c) + side]
+                await_bytes(other, sem_sw.at[s - 1, hq, side])
+                await_bytes(other, sem_sw_s.at[s - 1, hq, side])
 
     eye = identity(order)
     on = identity(128)
@@ -195,11 +193,18 @@
     def one_round(s):
         h0[...], l0[...] = load_pair(s, p)
         pair = (h0[...], l0[...])
-        gram = dot3(pair, pair, NT)
+        upper = dot3((h0[:half], l0[:half]), pair, NT)
+        lower = dot3((h0[half:], l0[half:]), (h0[half:], l0[half:]), NT)
+
+        def gram_tile(i, j):
+            at = 128 * i if i < 2 else 128 * i - half
+            source, shift = (upper, 0) if i < 2 else (lower, half)
+            return source[at:at + 128, 128 * j - shift:128 * j - shift + 128]
+
         for n, (i, j) in enumerate(TILES):
-            tile = gram[128 * i:128 * i + 128, 128 * j:128 * j + 128]
+            tile = gram_tile(i, j)
             if i == j:
-                second = gram[128 * i + 128:128 * i + 256, 128 * i + 128:128 * i + 256]
+                second = gram_tile(i + 1, i + 1)
                 tile = jnp.where(column_ids >= row_ids, tile, second)
                 D[s, i // 2:i // 2 + 1, :] = jnp.sum(jnp.where(on, second, 0.0), axis=0, keepdims=True)
             E[s, pl.ds(128 * n, 128), :] = tile
@@ -313,10 +318,10 @@
             h0[...], l0[...] = split(2.0 * inverse - jnp.where(eye, 1.0, 0.0))
             q = 2 * hq + c
             h1[...], l1[...] = load_pair(s, q)
-            turned = dot3((h0[...], l0[...]), (h1[...], l1[...]))
             for side in range(2):
-                S[s + 1][2 * q + side] = turned[half * side:half * side + half]
-            swap(s + 1, hq).start()
+                part_of = pl.ds(half * side, half)
+                S[s + 1][2 * q + side] = dot3((h0[part_of, :], l0[part_of, :]), (h1[...], l1[...]))
+                swap(s + 1, hq, side).start()
             return c2
 
         lax.fori_loop(0, 2, rotate, 0)
@@ -357,7 +362,7 @@
             pltpu.VMEM(full, F32), pltpu.VMEM(full, F32),
             pltpu.VMEM(full, BF16), pltpu.VMEM(full, BF16), pltpu.VMEM(full, BF16), pltpu.VMEM(full, BF16),
             pltpu.VMEM(full, BF16), pltpu.VMEM(full, BF16),
-            dma((2,)), dma((2,)), dma((2, 2)), dma((2,)), dma((2 * n_row,)), dma, dma, dma, dma((2, 2)), dma((2, 2)), dma((2, 3)), dma((2, 3)), dma((2, 3, 2)), dma((2, 3, 2)),
+            dma((2,)), dma((2,)), dma((2, 2)), dma((2,)), dma((2 * n_row,)), dma, dma, dma, dma((2, 2, 2)), dma((2, 2, 2)), dma((2, 3)), dma((2, 3)), dma((2, 3, 2)), dma((2, 3, 2)),
         ],
         compiler_params=pltpu.CompilerParams(
             collective_id=0, has_side_effects=True, vmem_limit_bytes=32 * 1024 * 1024),

time: 106 us -> 105 us (level)
  no operation moved by 1% of the time
where the time goes in v5:
time: 105 us
  Pallas kernels  105 us (100%)
    pallas_call x1, Pallas kernels, on_device(): pl.pallas_call(functools.partial(kernel, n_row), out_shape=jax.ShapeDtype...  104 us

profile of v5, /device:TPU:1, one launch (start us, length us, event | category | flops | bytes accessed | tf_op | source)
XLA Modules:
  0.0 104.8 jit_solution(11666725368697472546)
XLA Ops:
  0.0 103.8 %shard_map.28.blocks = f32[512,512]{1,0:T(8,128)S(1)} custom-call(s32[2,8]{1,0:T(2,128)} %plan.1, f32[16,1,16384]{2,1,0:T(1,128)} %snap.1), custom_call_target="tpu_custom_call" | custom-call | tf_op jit(solution)/shard_map/pallas_call | solution.py:350
  103.8 1.0 shard_map.29

commit v6 on v5

--- a/solution.py
+++ b/solution.py
@@ -15,7 +15,7 @@
 TILES = [(i, j) for i in range(4) for j in range(i + 1, 4)] + [(0, 0), (2, 2)]
 TILE_ROWS = 128 * len(TILES)
 PIECES = (8, 8, 16)
-ORDER = [(2, PIECES[2]), (0, PIECES[0]), (1, PIECES[1])]
+ORDER = [(2, PIECES[2]), (1, PIECES[1]), (0, PIECES[0])]
 
 
 def dot(left, right, dims=NN):

time: 105 us -> 105 us (level)
  no operation moved by 1% of the time
where the time goes in v6:
time: 105 us
  Pallas kernels  105 us (100%)
    pallas_call x1, Pallas kernels, on_device(): pl.pallas_call(functools.partial(kernel, n_row), out_shape=jax.ShapeDtype...  104 us

profile of v6, /device:TPU:1, one launch (start us, length us, event | category | flops | bytes accessed | tf_op | source)
XLA Modules:
  0.0 104.7 jit_solution(13846937855720380473)
XLA Ops:
  0.0 103.7 %shard_map.28.blocks = f32[512,512]{1,0:T(8,128)S(1)} custom-call(s32[2,8]{1,0:T(2,128)} %plan.1, f32[16,1,16384]{2,1,0:T(1,128)} %snap.1), custom_call_target="tpu_custom_call" | custom-call | tf_op jit(solution)/shard_map/pallas_call | solution.py:350
  103.7 1.0 shard_map.29
